TPU v7x, 512 devices: a whole 4x4x16 slice. The times are simulated.
512 devices in a mesh: row: 16 (over x, y), col: 32 (over z, core).
Axes of the slice: x: 4, y: 4, z: 16, core: 2. Of those that a mesh axis runs over, the one named last changes fastest.
Arguments:
- front: bfloat16 [16384, 16384], P('row', 'col'), may hold values from -0.046875 to 0.046875
- diag_inverse: float32 [128, 128, 128], P('row'), may hold values from -0.25 to 1.5
- load: float32 [8, 16384], P(None, 'row'), may hold values from -6 to 6
- panel_order: int32 [128], replicated, may hold values from 0 to 127, each once
- tie: float32 [32, 16384], P('col', 'row'), may hold values from 0.5 to 1.5
- mass: float32 [32, 16384], P('col', 'row'), may hold values from 0.5 to 6
- modes: bfloat16 [1024, 32, 16384], P(None, 'col', 'row'), may hold values from -0.0234375 to 0.0234375
Outputs:
- front_solution: float32 [8, 16384], P(None, 'row')
- residual_vectors: float32 [8, 32, 16384], P(None, 'col', 'row')
All inputs are finite; a program needn't handle non-finite values.
Results may differ from a plain program's by a relative error of at most 0.0049.
Values may be sent and summed in bfloat16 or wider, within the bound.
No kernel may reach another device: no remote copies, remote signals or barrier semaphores. Data moves between devices by JAX's collectives and lax.ppermute only.
A program may use at most 64 MiB of HBM per device.

v0:
```python
import jax
import jax.numpy as jnp
from jax import lax
from jax.sharding import PartitionSpec as P

LEVELS = 4
highest = lax.Precision.HIGHEST


def on_device(front, diag_inverse, load, panel_order, tie, mass, modes):
    vectors = load.shape[0]
    block_size = diag_inverse.shape[1]
    local_panels = diag_inverse.shape[0]
    rows_local = front.shape[0]
    cols_local = front.shape[1]
    panels = panel_order.shape[0]
    row_at = lax.axis_index("row")
    col_at = lax.axis_index("col")
    counting = jnp.arange(panels, dtype=jnp.int32)
    matches = panel_order[:, None] == counting[None, :]
    ranks = jnp.sum(jnp.where(matches, counting[:, None], 0), axis=0)
    levels_of = ranks // (panels // LEVELS)
    position_level = jnp.repeat(levels_of, block_size)
    row_level = lax.dynamic_slice_in_dim(position_level, row_at * rows_local, rows_local, 0)
    pending = jnp.zeros((vectors, rows_local), jnp.float32)
    forward_out = jnp.zeros((vectors, rows_local), jnp.float32)
    for level in range(LEVELS):
        if level > 0:
            total_sum = lax.psum(pending, "col")
        else:
            total_sum = pending
        remain = (load - total_sum).reshape(vectors, local_panels, block_size)
        candidate = jnp.einsum("vpj,pij->vpi", remain, diag_inverse, precision=highest).reshape(
            vectors, rows_local
        )
        chosen = row_level[None, :] == level
        forward_out = jnp.where(chosen, candidate, forward_out)
        if level < LEVELS - 1:
            fresh = jnp.where(chosen, forward_out, 0.0).astype(jnp.bfloat16)
            whole = lax.all_gather(fresh, "row", axis=1, tiled=True)
            mine = lax.dynamic_slice_in_dim(whole, col_at * cols_local, cols_local, 1)
            pending = pending + jnp.dot(mine, front.T, preferred_element_type=jnp.float32)
    back_pending = jnp.zeros((vectors, cols_local), jnp.float32)
    back_out = jnp.zeros((vectors, rows_local), jnp.float32)
    for level in reversed(range(LEVELS)):
        if level < LEVELS - 1:
            column_sum = lax.psum(back_pending, "row")
            full_sum = lax.all_gather(column_sum, "col", axis=1, tiled=True)
            here = lax.dynamic_slice_in_dim(full_sum, row_at * rows_local, rows_local, 1)
        else:
            here = jnp.zeros((vectors, rows_local), jnp.float32)
        remain = (forward_out - here).reshape(vectors, local_panels, block_size)
        candidate = jnp.einsum("vpj,pji->vpi", remain, diag_inverse, precision=highest).reshape(
            vectors, rows_local
        )
        chosen = row_level[None, :] == level
        back_out = jnp.where(chosen, candidate, back_out)
        if level > 0:
            fresh = jnp.where(chosen, back_out, 0.0).astype(jnp.bfloat16)
            back_pending = back_pending + jnp.dot(fresh, front, preferred_element_type=jnp.float32)
    static = tie[None, :, :] * back_out[:, None, :]
    weighted = (mass[None, :, :] * static).astype(jnp.bfloat16).reshape(vectors, -1)
    mode_rows = modes.reshape(modes.shape[0], -1)
    partial_coords = lax.dot_general(
        weighted, mode_rows, (((1,), (1,)), ((), ())), preferred_element_type=jnp.float32
    )
    coords = lax.psum(partial_coords, ("row", "col"))
    correction = jnp.dot(coords.astype(jnp.bfloat16), mode_rows, preferred_element_type=jnp.float32)
    return (back_out, static - correction.reshape(static.shape))


def solution(mesh):
    in_specs = (
        P("row", "col"),
        P("row", None, None),
        P(None, "row"),
        P(),
        P("col", "row"),
        P("col", "row"),
        P(None, "col", "row"),
    )
    out_specs = (P(None, "row"), P(None, "col", "row"))
    return jax.shard_map(
        on_device, mesh=mesh, in_specs=in_specs, out_specs=out_specs, check_vma=False
    )
```

profile of v0, /device:TPU:1, one launch (start us, length us, event | category | flops | bytes accessed | tf_op | source)
XLA Modules:
  0.0 765.4 jit_solution(5559178636949547583)
XLA Ops:
  0.6 0.0 copy-start
  0.6 0.0 copy-start.1
  0.7 0.0 copy-start.2
  0.7 0.9 select_reduce_fusion
  1.6 0.1 broadcast_bitcast_fusion
  1.7 2.0 select_convert_fusion.5
  3.7 19.7 %all_gather.18 = bf16[8,16384]{1,0:T(8,128)(2,1)S(1)} all-gather(bf16[8,1024]{1,0:T(8,128)(2,1)S(1)} %get-tuple-element.14), channel_id=1, replica_groups=mesh['row'=16,'col'=32] {'row'}, dimensions={1}, use_global_device_ids=true | all-gather | bytes 278528 | tf_op jit(solution)/shard_map/all_gather | solution.py:40
  23.3 1.6 fusion.64
  24.9 99.0 %psum.49 = f32[8,1024]{1,0:T(8,128)S(1)} all-reduce(f32[8,1024]{1,0:T(8,128)S(1)} %fusion.64), channel_id=1, replica_groups=mesh['row'=16,'col'=32] {'col'}, use_global_device_ids=true, to_apply=%region_1.2 | all-reduce | flops 8192 | bytes 65536 | tf_op jit(solution)/shard_map/psum | solution.py:29
  123.9 0.0 copy-done.2
  123.9 2.0 select_convert_fusion.4
  125.9 17.9 %all_gather.19 = bf16[8,16384]{1,0:T(8,128)(2,1)S(1)} all-gather(bf16[8,1024]{1,0:T(8,128)(2,1)S(1)} %get-tuple-element.8), channel_id=1, replica_groups=mesh['row'=16,'col'=32] {'row'}, dimensions={1}, use_global_device_ids=true | all-gather | bytes 278528 | tf_op jit(solution)/shard_map/all_gather | solution.py:40
  143.8 0.0 copy-done.1
  143.8 0.4 convolution_add_fusion.1
  144.2 95.2 %psum.50 = f32[8,1024]{1,0:T(8,128)S(1)} all-reduce(f32[8,1024]{1,0:T(8,128)S(1)} %convolution_add_fusion.1), channel_id=1, replica_groups=mesh['row'=16,'col'=32] {'col'}, use_global_device_ids=true, to_apply=%region_2.3 | all-reduce | flops 8192 | bytes 65536 | tf_op jit(solution)/shard_map/psum | solution.py:29
  239.4 2.0 select_convert_fusion.3
  241.4 16.6 %all_gather.20 = bf16[8,16384]{1,0:T(8,128)(2,1)S(1)} all-gather(bf16[8,1024]{1,0:T(8,128)(2,1)S(1)} %get-tuple-element.17), channel_id=1, replica_groups=mesh['row'=16,'col'=32] {'row'}, dimensions={1}, use_global_device_ids=true | all-gather | bytes 278528 | tf_op jit(solution)/shard_map/all_gather | solution.py:40
  258.0 0.4 convolution_add_fusion
  258.4 94.9 %psum.51 = f32[8,1024]{1,0:T(8,128)S(1)} all-reduce(f32[8,1024]{1,0:T(8,128)S(1)} %convolution_add_fusion), channel_id=1, replica_groups=mesh['row'=16,'col'=32] {'col'}, use_global_device_ids=true, to_apply=%region_3.4 | all-reduce | flops 8192 | bytes 65536 | tf_op jit(solution)/shard_map/psum | solution.py:29
  353.3 2.0 bitcast_select_fusion.5
  355.3 1.6 fusion.22
  356.9 0.2 fusion.40
  357.1 58.2 %psum.52 = f32[8,512]{1,0:T(8,128)S(1)} all-reduce(f32[8,512]{1,0:T(8,128)S(1)} %fusion.40), channel_id=1, replica_groups=mesh['row'=16,'col'=32] {'row'}, use_global_device_ids=true, to_apply=%region_4.5 | all-reduce | flops 4096 | bytes 32768 | tf_op jit(solution)/shard_map/psum | solution.py:47
  415.3 45.4 %all_gather.21 = f32[8,16384]{1,0:T(8,128)S(1)} all-gather(f32[8,512]{1,0:T(8,128)S(1)} %psum.52), channel_id=1, replica_groups=mesh['row'=16,'col'=32] {'col'}, dimensions={1}, use_global_device_ids=true | all-gather | bytes 540672 | tf_op jit(solution)/shard_map/all_gather | solution.py:48
  460.8 1.6 bitcast_select_fusion.3
  462.3 0.2 convolution_add_fusion.3
  462.6 0.0 copy-start.4
  462.6 0.0 copy-start.5
  462.6 55.9 %psum.53 = f32[8,512]{1,0:T(8,128)S(1)} all-reduce(f32[8,512]{1,0:T(8,128)S(1)} %convolution_add_fusion.3), channel_id=1, replica_groups=mesh['row'=16,'col'=32] {'row'}, use_global_device_ids=true, to_apply=%region_5.6 | all-reduce | flops 4096 | bytes 32768 | tf_op jit(solution)/shard_map/psum | solution.py:47
  518.5 44.6 %all_gather.22 = f32[8,16384]{1,0:T(8,128)S(1)} all-gather(f32[8,512]{1,0:T(8,128)S(1)} %psum.53), channel_id=1, replica_groups=mesh['row'=16,'col'=32] {'col'}, dimensions={1}, use_global_device_ids=true | all-gather | bytes 540672 | tf_op jit(solution)/shard_map/all_gather | solution.py:48
  563.1 1.6 fusion.18
  564.6 0.2 convolution_add_fusion.2
  564.9 55.8 %psum.54 = f32[8,512]{1,0:T(8,128)S(1)} all-reduce(f32[8,512]{1,0:T(8,128)S(1)} %convolution_add_fusion.2), channel_id=1, replica_groups=mesh['row'=16,'col'=32] {'row'}, use_global_device_ids=true, to_apply=%region_6.7 | all-reduce | flops 4096 | bytes 32768 | tf_op jit(solution)/shard_map/psum | solution.py:47
  620.6 42.0 %all_gather.23 = f32[8,16384]{1,0:T(8,128)S(1)} all-gather(f32[8,512]{1,0:T(8,128)S(1)} %psum.54), channel_id=1, replica_groups=mesh['row'=16,'col'=32] {'col'}, dimensions={1}, use_global_device_ids=true | all-gather | bytes 540672 | tf_op jit(solution)/shard_map/all_gather | solution.py:48
  662.6 1.6 bitcast_select_fusion.1
  664.2 0.0 copy-start.3
  664.2 0.0 copy-done
  664.2 0.0 copy-done.4
  664.2 0.0 copy-done.5
  664.2 0.6 fusion.2
  664.8 99.5 %psum.55 = bf16[8,1024]{1,0:T(8,128)(2,1)S(1)} all-reduce(f32[8,1024]{1,0:T(8,128)S(1)} %fusion.2), channel_id=1, replica_groups=mesh['row'=16,'col'=32] {'row','col'}, use_global_device_ids=true, to_apply=%region_7.8 | all-reduce | flops 8192 | bytes 49152 | tf_op jit(solution)/shard_map/psum | solution.py:67
  764.4 0.4 fusion.7
  764.8 0.0 copy-done.3
  764.8 0.7 copy.11
  (2 shorter events, 0.0 us)
Async XLA Ops:
  0.6 663.6 %copy-start = (bf16[1024,1,1024]{2,0,1:T(8,128)(2,1)S(1)}, bf16[1024,1,1024]{2,0,1:T(8,128)(2,1)}, u32[]{:S(2)}) copy-start(bf16[1024,1,1024]{2,0,1:T(8,128)(2,1)} %param.13) | copy-start | bytes 6291460
  0.6 143.2 %copy-start.1 = (bf16[1024,512]{1,0:T(8,128)(2,1)S(1)}, bf16[1024,512]{1,0:T(8,128)(2,1)}, u32[]{:S(2)}) copy-start(bf16[1024,512]{1,0:T(8,128)(2,1)} %param.7) | copy-start | bytes 3145732
  0.7 123.3 %copy-start.2 = (f32[8,1024]{1,0:T(8,128)S(1)}, f32[8,1024]{1,0:T(8,128)}, u32[]{:S(2)}) copy-start(f32[8,1024]{1,0:T(8,128)} %param.9) | copy-start | bytes 98308
  462.6 201.6 %copy-start.4 = (f32[1,1024]{1,0:T(1,128)S(1)}, f32[1,1024]{1,0:T(1,128)}, u32[]{:S(2)}) copy-start(f32[1,1024]{1,0:T(1,128)} %param.11) | copy-start | bytes 12292
  462.6 201.6 %copy-start.5 = (f32[1,1024]{1,0:T(1,128)S(1)}, f32[1,1024]{1,0:T(1,128)}, u32[]{:S(2)}) copy-start(f32[1,1024]{1,0:T(1,128)} %param.12) | copy-start | bytes 12292
  664.2 100.6 %copy-start.3 = (f32[8,1024]{1,0:T(8,128)}, f32[8,1024]{1,0:T(8,128)S(1)}, u32[]{:S(2)}) copy-start(f32[8,1024]{1,0:T(8,128)S(1)} %get-tuple-element.23) | copy-start | bytes 98308
where the time goes:
time: 766 us; the launch traced here: 765 us
  blocking collectives  745 us (97%)
  matrix products  18.2 us (2%)
    psum x3, blocking collectives, on_device(): total_sum = lax.psum(pending, 'col')  289 us
    psum x3, blocking collectives, on_device(): column_sum = lax.psum(back_pending, 'row')  170 us
    all_gather x3, blocking collectives, on_device(): full_sum = lax.all_gather(column_sum, 'col', axis=1, tiled=True)  132 us
    psum x1, blocking collectives, on_device(): coords = lax.psum(partial_coords, ('row', 'col'))  99.5 us
    all_gather x3, blocking collectives, on_device(): whole = lax.all_gather(fresh, 'row', axis=1, tiled=True)  54.2 us

commit v1 on v0

--- a/solution.py
+++ b/solution.py
@@ -64,7 +64,8 @@
     partial_coords = lax.dot_general(
         weighted, mode_rows, (((1,), (1,)), ((), ())), preferred_element_type=jnp.float32
     )
-    coords = lax.psum(partial_coords, ("row", "col"))
+    switch_lane_all = lambda u: lax.psum(lax.psum(u, axis_name="row"), "col")
+    coords = switch_lane_all(partial_coords)
     correction = jnp.dot(coords.astype(jnp.bfloat16), mode_rows, preferred_element_type=jnp.float32)
     return (back_out, static - correction.reshape(static.shape))
 

time: 766 us -> 823 us (1.074)
  blocking collectives: 745 us -> 801 us
    psum x1 -> x2, blocking collectives: 99.5 us -> 156 us  [on_device(): switch_lane_all = lambda u: lax.psum(lax.psum(u, axis_name='row'), 'col')]
where the time goes in v1:
time: 823 us; the launch traced here: 822 us
  blocking collectives  801 us (97%)
  matrix products  18.2 us (2%)
    psum x3, blocking collectives, on_device(): total_sum = lax.psum(pending, 'col')  289 us
    psum x3, blocking collectives, on_device(): column_sum = lax.psum(back_pending, 'row')  170 us
    psum x2, blocking collectives, on_device(): switch_lane_all = lambda u: lax.psum(lax.psum(u, axis_name='row'), 'col')  156 us
    all_gather x3, blocking collectives, on_device(): full_sum = lax.all_gather(column_sum, 'col', axis=1, tiled=True)  132 us
    all_gather x3, blocking collectives, on_device(): whole = lax.all_gather(fresh, 'row', axis=1, tiled=True)  54.2 us

profile of v1, /device:TPU:1, one launch (start us, length us, event | category | flops | bytes accessed | tf_op | source)
XLA Modules:
  0.0 822.1 jit_solution(5408746188882743132)
XLA Ops:
  0.6 0.0 copy-start
  0.6 0.0 copy-start.1
  0.7 0.0 copy-start.2
  0.7 0.9 select_reduce_fusion
  1.6 0.1 broadcast_bitcast_fusion
  1.7 2.0 select_convert_fusion.5
  3.7 19.7 %all_gather.18 = bf16[8,16384]{1,0:T(8,128)(2,1)S(1)} all-gather(bf16[8,1024]{1,0:T(8,128)(2,1)S(1)} %get-tuple-element.14), channel_id=1, replica_groups=mesh['row'=16,'col'=32] {'row'}, dimensions={1}, use_global_device_ids=true | all-gather | bytes 278528 | tf_op jit(solution)/shard_map/all_gather | solution.py:40
  23.3 1.6 fusion.64
  24.9 99.0 %psum.56 = f32[8,1024]{1,0:T(8,128)S(1)} all-reduce(f32[8,1024]{1,0:T(8,128)S(1)} %fusion.64), channel_id=1, replica_groups=mesh['row'=16,'col'=32] {'col'}, use_global_device_ids=true, to_apply=%region_1.2 | all-reduce | flops 8192 | bytes 65536 | tf_op jit(solution)/shard_map/psum | solution.py:29
  123.9 0.0 copy-done.2
  123.9 2.0 select_convert_fusion.4
  125.9 17.9 %all_gather.19 = bf16[8,16384]{1,0:T(8,128)(2,1)S(1)} all-gather(bf16[8,1024]{1,0:T(8,128)(2,1)S(1)} %get-tuple-element.8), channel_id=1, replica_groups=mesh['row'=16,'col'=32] {'row'}, dimensions={1}, use_global_device_ids=true | all-gather | bytes 278528 | tf_op jit(solution)/shard_map/all_gather | solution.py:40
  143.8 0.0 copy-done.1
  143.8 0.4 convolution_add_fusion.1
  144.2 95.2 %psum.57 = f32[8,1024]{1,0:T(8,128)S(1)} all-reduce(f32[8,1024]{1,0:T(8,128)S(1)} %convolution_add_fusion.1), channel_id=1, replica_groups=mesh['row'=16,'col'=32] {'col'}, use_global_device_ids=true, to_apply=%region_2.3 | all-reduce | flops 8192 | bytes 65536 | tf_op jit(solution)/shard_map/psum | solution.py:29
  239.4 2.0 select_convert_fusion.3
  241.4 16.6 %all_gather.20 = bf16[8,16384]{1,0:T(8,128)(2,1)S(1)} all-gather(bf16[8,1024]{1,0:T(8,128)(2,1)S(1)} %get-tuple-element.17), channel_id=1, replica_groups=mesh['row'=16,'col'=32] {'row'}, dimensions={1}, use_global_device_ids=true | all-gather | bytes 278528 | tf_op jit(solution)/shard_map/all_gather | solution.py:40
  258.0 0.4 convolution_add_fusion
  258.4 94.9 %psum.58 = f32[8,1024]{1,0:T(8,128)S(1)} all-reduce(f32[8,1024]{1,0:T(8,128)S(1)} %convolution_add_fusion), channel_id=1, replica_groups=mesh['row'=16,'col'=32] {'col'}, use_global_device_ids=true, to_apply=%region_3.4 | all-reduce | flops 8192 | bytes 65536 | tf_op jit(solution)/shard_map/psum | solution.py:29
  353.3 2.0 bitcast_select_fusion.5
  355.3 1.6 fusion.22
  356.9 0.2 fusion.40
  357.1 58.2 %psum.59 = f32[8,512]{1,0:T(8,128)S(1)} all-reduce(f32[8,512]{1,0:T(8,128)S(1)} %fusion.40), channel_id=1, replica_groups=mesh['row'=16,'col'=32] {'row'}, use_global_device_ids=true, to_apply=%region_4.5 | all-reduce | flops 4096 | bytes 32768 | tf_op jit(solution)/shard_map/psum | solution.py:47
  415.3 45.4 %all_gather.21 = f32[8,16384]{1,0:T(8,128)S(1)} all-gather(f32[8,512]{1,0:T(8,128)S(1)} %psum.59), channel_id=1, replica_groups=mesh['row'=16,'col'=32] {'col'}, dimensions={1}, use_global_device_ids=true | all-gather | bytes 540672 | tf_op jit(solution)/shard_map/all_gather | solution.py:48
  460.8 1.6 bitcast_select_fusion.3
  462.3 0.2 convolution_add_fusion.3
  462.6 0.0 copy-start.4
  462.6 0.0 copy-start.5
  462.6 55.9 %psum.60 = f32[8,512]{1,0:T(8,128)S(1)} all-reduce(f32[8,512]{1,0:T(8,128)S(1)} %convolution_add_fusion.3), channel_id=1, replica_groups=mesh['row'=16,'col'=32] {'row'}, use_global_device_ids=true, to_apply=%region_5.6 | all-reduce | flops 4096 | bytes 32768 | tf_op jit(solution)/shard_map/psum | solution.py:47
  518.5 44.6 %all_gather.22 = f32[8,16384]{1,0:T(8,128)S(1)} all-gather(f32[8,512]{1,0:T(8,128)S(1)} %psum.60), channel_id=1, replica_groups=mesh['row'=16,'col'=32] {'col'}, dimensions={1}, use_global_device_ids=true | all-gather | bytes 540672 | tf_op jit(solution)/shard_map/all_gather | solution.py:48
  563.1 1.6 fusion.18
  564.6 0.2 convolution_add_fusion.2
  564.9 55.8 %psum.61 = f32[8,512]{1,0:T(8,128)S(1)} all-reduce(f32[8,512]{1,0:T(8,128)S(1)} %convolution_add_fusion.2), channel_id=1, replica_groups=mesh['row'=16,'col'=32] {'row'}, use_global_device_ids=true, to_apply=%region_6.7 | all-reduce | flops 4096 | bytes 32768 | tf_op jit(solution)/shard_map/psum | solution.py:47
  620.6 42.0 %all_gather.23 = f32[8,16384]{1,0:T(8,128)S(1)} all-gather(f32[8,512]{1,0:T(8,128)S(1)} %psum.61), channel_id=1, replica_groups=mesh['row'=16,'col'=32] {'col'}, dimensions={1}, use_global_device_ids=true | all-gather | bytes 540672 | tf_op jit(solution)/shard_map/all_gather | solution.py:48
  662.6 1.6 bitcast_select_fusion.1
  664.2 0.0 copy-start.3
  664.2 0.0 copy-done
  664.2 0.0 copy-done.4
  664.2 0.0 copy-done.5
  664.2 0.6 fusion.2
  664.8 55.8 %psum.62 = f32[8,1024]{1,0:T(8,128)S(1)} all-reduce(f32[8,1024]{1,0:T(8,128)S(1)} %fusion.2), channel_id=1, replica_groups=mesh['row'=16,'col'=32] {'row'}, use_global_device_ids=true, to_apply=%region_7.8 | all-reduce | flops 8192 | bytes 65536 | tf_op jit(solution)/shard_map/psum | solution.py:67
  720.6 100.4 %psum.63 = bf16[8,1024]{1,0:T(8,128)(2,1)S(1)} all-reduce(f32[8,1024]{1,0:T(8,128)S(1)} %psum.62), channel_id=1, replica_groups=mesh['row'=16,'col'=32] {'col'}, use_global_device_ids=true, to_apply=%region_8.9 | all-reduce | flops 8192 | bytes 49152 | tf_op jit(solution)/shard_map/psum | solution.py:67
  821.0 0.4 fusion.7
  821.4 0.0 copy-done.3
  821.4 0.7 copy.11
  (2 shorter events, 0.0 us)
Async XLA Ops:
  0.6 663.6 %copy-start = (bf16[1024,1,1024]{2,0,1:T(8,128)(2,1)S(1)}, bf16[1024,1,1024]{2,0,1:T(8,128)(2,1)}, u32[]{:S(2)}) copy-start(bf16[1024,1,1024]{2,0,1:T(8,128)(2,1)} %param.13) | copy-start | bytes 6291460
  0.6 143.2 %copy-start.1 = (bf16[1024,512]{1,0:T(8,128)(2,1)S(1)}, bf16[1024,512]{1,0:T(8,128)(2,1)}, u32[]{:S(2)}) copy-start(bf16[1024,512]{1,0:T(8,128)(2,1)} %param.7) | copy-start | bytes 3145732
  0.7 123.3 %copy-start.2 = (f32[8,1024]{1,0:T(8,128)S(1)}, f32[8,1024]{1,0:T(8,128)}, u32[]{:S(2)}) copy-start(f32[8,1024]{1,0:T(8,128)} %param.9) | copy-start | bytes 98308
  462.6 201.6 %copy-start.4 = (f32[1,1024]{1,0:T(1,128)S(1)}, f32[1,1024]{1,0:T(1,128)}, u32[]{:S(2)}) copy-start(f32[1,1024]{1,0:T(1,128)} %param.11) | copy-start | bytes 12292
  462.6 201.6 %copy-start.5 = (f32[1,1024]{1,0:T(1,128)S(1)}, f32[1,1024]{1,0:T(1,128)}, u32[]{:S(2)}) copy-start(f32[1,1024]{1,0:T(1,128)} %param.12) | copy-start | bytes 12292
  664.2 157.2 %copy-start.3 = (f32[8,1024]{1,0:T(8,128)}, f32[8,1024]{1,0:T(8,128)S(1)}, u32[]{:S(2)}) copy-start(f32[8,1024]{1,0:T(8,128)S(1)} %get-tuple-element.23) | copy-start | bytes 98308
